TPU v7x, 32 devices: a whole 2x2x4 slice. The times are simulated.
32 devices in a mesh: dp: 8 (over y, x, core), dap: 4 (over z).
Axes of the slice: x: 2, y: 2, z: 4, core: 2. Of those that a mesh axis runs over, the one named last changes fastest.
Arguments:
- pair_act: bfloat16 [8, 128, 128, 128], P('dp', 'dap'), may hold values from -6 to 6
- pair_cot: bfloat16 [8, 128, 128, 128], P('dp', 'dap'), may hold values from -6 to 6
- in_gain: float32 [128], replicated, may hold values from 0.25 to 1.75
- in_bias: float32 [128], replicated, may hold values from -3 to 3
- proj_weight: bfloat16 [128, 512], replicated, may hold values from -0.5 to 0.5
- gate_weight: bfloat16 [128, 128], replicated, may hold values from -0.5 to 0.5
- out_gain: float32 [128], replicated, may hold values from 0.25 to 1.75
- out_bias: float32 [128], replicated, may hold values from -3 to 3
- out_weight: bfloat16 [128, 128], replicated, may hold values from -0.5 to 0.5
Outputs:
- update: bfloat16 [8, 128, 128, 128], P('dp', 'dap')
- pair_grad: bfloat16 [8, 128, 128, 128], P('dp', 'dap')
- proj_grad: float32 [128, 512], replicated
- gate_grad: float32 [128, 128], replicated
- out_grad: float32 [128, 128], replicated
- in_norm_grad: float32 [2, 128], replicated
- out_norm_grad: float32 [2, 128], replicated
All inputs are finite; a program needn't handle non-finite values.
Results may differ from a plain program's by a relative error of at most 0.0084.
Values may be sent and summed in bfloat16 or wider, within the bound.
A program may use at most 64 MiB of HBM per device.

v0:
```python
import jax
import jax.numpy as jnp
from jax import lax
from jax.sharding import PartitionSpec as P

epsilon = 1e-05


def norm_rows(values, along):
    row_mean = jnp.mean(values, axis=along, keepdims=True)
    centred = values - row_mean
    row_var = jnp.mean(centred * centred, axis=along, keepdims=True)
    inv_std = lax.rsqrt(row_var + epsilon)
    return (centred * inv_std, inv_std)


def norm_back(grad_hat, x_hat, inv_std, along):
    first = jnp.mean(grad_hat, axis=along, keepdims=True)
    second = jnp.mean(grad_hat * x_hat, axis=along, keepdims=True)
    return (grad_hat - first - x_hat * second) * inv_std


def backward_pieces(piece_d, piece_l, piece_r):
    back_l = jnp.einsum(
        "zhij,zhjk->zhik", piece_d, piece_r, preferred_element_type=jnp.float32
    ).astype(jnp.bfloat16)
    back_r = jnp.einsum(
        "zhij,zhik->zhjk", piece_d, piece_l, preferred_element_type=jnp.float32
    ).astype(jnp.bfloat16)
    return (back_l, back_r)


def shards(
    pair_act, pair_cot, in_gain, in_bias, proj_weight, gate_weight, out_gain, out_bias, out_weight
):
    f32 = jnp.float32
    bf16 = jnp.bfloat16
    groups = lax.axis_size("dap")
    row_count = pair_act.shape[1]
    crop_len = pair_act.shape[2]
    channels = pair_act.shape[3]
    hidden_w = out_weight.shape[0]
    per_dev = hidden_w // groups
    cell_count = row_count * crop_len
    scale = 1.0 / crop_len
    flat_act = pair_act.reshape(cell_count, channels).astype(f32)
    in_hat, in_inv = norm_rows(flat_act, 1)
    normed = (in_hat * in_gain + in_bias).astype(bf16)
    projected = jnp.einsum("mc,ch->hm", normed, proj_weight, preferred_element_type=f32)
    pre_ag = projected[0:hidden_w]
    pre_ap = projected[hidden_w : 2 * hidden_w]
    pre_bg = projected[2 * hidden_w : 3 * hidden_w]
    pre_bp = projected[3 * hidden_w : 4 * hidden_w]
    sig_a = jax.nn.sigmoid(pre_ag)
    sig_b = jax.nn.sigmoid(pre_bg)
    left_act = (sig_a * pre_ap).astype(bf16).reshape(groups, per_dev, row_count, crop_len)
    right_act = (sig_b * pre_bp).astype(bf16).reshape(groups, per_dev, row_count, crop_len)
    piece_l = lax.all_to_all(left_act, "dap", split_axis=0, concat_axis=2, tiled=True)
    piece_r = lax.all_to_all(right_act, "dap", split_axis=0, concat_axis=2, tiled=True)
    product = jnp.einsum("zhik,zhjk->zhij", piece_l, piece_r, preferred_element_type=f32).astype(
        bf16
    )
    returned = lax.all_to_all(product, "dap", split_axis=2, concat_axis=0, tiled=True)
    tri_out = returned.reshape(hidden_w, cell_count)
    tri_hat, tri_inv = norm_rows(tri_out.astype(f32), 0)
    tri_norm = (tri_hat * out_gain[:, None] + out_bias[:, None]).astype(bf16)
    gate_val = jax.nn.sigmoid(jnp.dot(normed, gate_weight, preferred_element_type=f32))
    mixed = jnp.einsum("hm,hc->mc", tri_norm, out_weight, preferred_element_type=f32)
    update = (gate_val * mixed).astype(bf16).reshape(1, row_count, crop_len, channels)
    cot_flat = pair_cot.reshape(cell_count, channels).astype(f32)
    d_mixed = (cot_flat * gate_val).astype(bf16)
    d_gate = (cot_flat * mixed * gate_val * (1.0 - gate_val)).astype(bf16)
    out_part = jnp.einsum("hm,mc->hc", tri_norm, d_mixed, preferred_element_type=f32) * scale
    gate_part = jnp.einsum("mc,md->cd", normed, d_gate, preferred_element_type=f32) * scale
    d_norm_out = jnp.einsum("mc,hc->hm", d_mixed, out_weight, preferred_element_type=f32)
    out_norm_part = (
        jnp.stack([jnp.sum(d_norm_out * tri_hat, axis=1), jnp.sum(d_norm_out, axis=1)]) * scale
    )
    d_tri = norm_back(d_norm_out * out_gain[:, None], tri_hat, tri_inv, 0).astype(bf16)
    d_tri = d_tri.reshape(groups, per_dev, row_count, crop_len)
    d_cols = lax.all_to_all(d_tri, "dap", split_axis=0, concat_axis=2, tiled=True)
    back_l, back_r = backward_pieces(d_cols, piece_l, piece_r)
    d_left, d_right = (
        lax.all_to_all(back_l, "dap", split_axis=2, concat_axis=0, tiled=True),
        lax.all_to_all(back_r, "dap", split_axis=2, concat_axis=0, tiled=True),
    )
    left_grad = d_left.reshape(hidden_w, cell_count).astype(f32)
    right_grad = d_right.reshape(hidden_w, cell_count).astype(f32)
    d_proj = jnp.concatenate(
        [
            left_grad * pre_ap * sig_a * (1.0 - sig_a),
            left_grad * sig_a,
            right_grad * pre_bp * sig_b * (1.0 - sig_b),
            right_grad * sig_b,
        ],
        axis=0,
    ).astype(bf16)
    proj_part = jnp.einsum("mc,hm->ch", normed, d_proj, preferred_element_type=f32) * scale
    d_normed = jnp.einsum(
        "hm,ch->mc", d_proj, proj_weight, preferred_element_type=f32
    ) + jnp.einsum("md,cd->mc", d_gate, gate_weight, preferred_element_type=f32)
    in_norm_part = (
        jnp.stack([jnp.sum(d_normed * in_hat, axis=0), jnp.sum(d_normed, axis=0)]) * scale
    )
    pair_grad = (
        norm_back(d_normed * in_gain, in_hat, in_inv, 1)
        .astype(bf16)
        .reshape(1, row_count, crop_len, channels)
    )
    proj_sum, gate_sum, out_sum, in_sum, outn_sum = lax.psum(
        (proj_part, gate_part, out_part, in_norm_part, out_norm_part), ("dp", "dap")
    )
    return (update, pair_grad, proj_sum, gate_sum, out_sum, in_sum, outn_sum)


def solution(mesh):
    placed = (
        P("dp", "dap", None, None),
        P("dp", "dap", None, None),
        P(),
        P(),
        P(),
        P(),
        P(),
        P(),
        P(),
    )
    return jax.shard_map(
        shards,
        mesh=mesh,
        in_specs=placed,
        out_specs=(P("dp", "dap", None, None), P("dp", "dap", None, None), P(), P(), P(), P(), P()),
        check_vma=False,
    )
```

profile of v0, /device:TPU:0, one launch (start us, length us, event | category | flops | bytes accessed | tf_op | source)
XLA Modules:
  0.0 383.8 jit_solution(13851624344998094155)
XLA Ops:
  7.2 1.7 convert_reduce_fusion
  8.9 2.3 multiply_reduce_fusion.3
  11.3 1.3 add_convert_fusion.1
  12.6 1.0 copy-done.5
  13.5 1.3 convolution_bitcast_fusion
  14.8 1.1 fusion.30
  15.9 2.1 copy-done.1
  18.1 1.2 copy.46
  19.3 6.3 %all-to-all-start.1 = ((bf16[4,32,32,128]{3,2,1,0:T(8,128)(2,1)}), bf16[4,32,32,128]{3,2,1,0:T(8,128)(2,1)S(1)}, u32[]{:S(2)}, u32[]{:S(2)}) async-start(bf16[4,32,32,128]{3,2,1,0:T(8,128)(2,1)} %bitcast.157), calls=%async_computation.1 | async-start | bytes 2097152 | tf_op jit(solution)/shard_map/all_to_all | solution.py:59
  25.6 1.2 copy.45
  26.8 24.5 %all-to-all-done.1 = bf16[4,32,32,128]{3,2,1,0:T(8,128)(2,1)S(1)} async-done(((bf16[4,32,32,128]{3,2,1,0:T(8,128)(2,1)}), bf16[4,32,32,128]{3,2,1,0:T(8,128)(2,1)S(1)}, u32[]{:S(2)}, u32[]{:S(2)}) %all-to-all-start.1) | async-done | bytes 1048608 | tf_op jit(solution)/shard_map/all_to_all | solution.py:59
  51.4 4.3 %all-to-all-start = ((bf16[4,32,32,128]{3,2,1,0:T(8,128)(2,1)}), bf16[4,32,32,128]{3,2,1,0:T(8,128)(2,1)}, u32[]{:S(2)}, u32[]{:S(2)}) async-start(bf16[4,32,32,128]{3,2,1,0:T(8,128)(2,1)} %bitcast.156), calls=%async_computation | async-start | bytes 2097152 | tf_op jit(solution)/shard_map/all_to_all | solution.py:58
  55.8 25.2 %all-to-all-done = bf16[4,32,32,128]{3,2,1,0:T(8,128)(2,1)} async-done(((bf16[4,32,32,128]{3,2,1,0:T(8,128)(2,1)}), bf16[4,32,32,128]{3,2,1,0:T(8,128)(2,1)}, u32[]{:S(2)}, u32[]{:S(2)}) %all-to-all-start) | async-done | bytes 1048608 | tf_op jit(solution)/shard_map/all_to_all | solution.py:58
  81.0 1.3 copy.32
  83.9 27.7 %all_to_all.72 = bf16[1,32,128,128]{3,1,0,2:T(8,128)(2,1)S(1)} all-to-all(bf16[1,32,128,128]{3,1,0,2:T(8,128)(2,1)S(1)} %copy.34), channel_id=1, replica_groups=mesh['dp'=8,'dap'=4] {'dap'}, dimensions={2} | all-to-all | bytes 2097152 | tf_op jit(solution)/shard_map/all_to_all | solution.py:63
  112.2 1.1 bitcast_reduce_fusion
  113.4 1.1 fusion.23
  114.5 3.0 copy.58
  117.5 1.9 copy.36
  119.4 2.3 add_convert_fusion
  121.8 1.0 copy-done.12
  124.3 2.7 fusion.6
  127.0 2.4 fusion.21
  129.4 1.3 copy-done.3
  130.8 4.1 %multiply_convert_fusion.1 = bf16[128,4096]{0,1:T(8,128)(2,1)} fusion(f32[4096,128]{1,0:T(8,128)S(1)} %get-tuple-element.34, f32[128,4096]{0,1:T(8,128)S(1)} %copy.36, f32[4096]{0:T(1024)S(1)} %get-tuple-element.36, f32[4096]{0:T(1024)S(1)} %get-tuple-element.37, f32[128]{0:T(128)S(1)} %copy-done.22, f32[4096]{0:T(1024)S(1)} %rsqrt_bitcast_fusion, ...), kind=kLoop, calls=%fused_computation.46 | loop fusion | flops 4194304 | bytes 5308928 | tf_op jit(solution)/shard_map/convert_element_type | solution.py:79
  134.8 1.5 copy.37
  136.6 27.8 %all_to_all.73 = bf16[4,32,32,128]{3,2,1,0:T(8,128)(2,1)S(1)} all-to-all(bf16[4,32,32,128]{3,2,1,0:T(8,128)(2,1)S(1)} %bitcast.159), channel_id=1, replica_groups=mesh['dp'=8,'dap'=4] {'dap'}, dimensions={0} | all-to-all | bytes 2097152 | tf_op jit(solution)/shard_map/all_to_all | solution.py:81
  165.0 1.7 copy.39
  166.6 4.3 %all-to-all-start.4 = ((bf16[1,32,128,128]{3,1,0,2:T(8,128)(2,1)}), bf16[1,32,128,128]{3,1,0,2:T(8,128)(2,1)}, u32[]{:S(2)}, u32[]{:S(2)}) async-start(bf16[1,32,128,128]{3,1,0,2:T(8,128)(2,1)} %copy.39), calls=%async_computation.4 | async-start | bytes 2097152 | tf_op jit(solution)/shard_map/all_to_all | solution.py:84
  171.4 1.7 copy.42
  173.1 22.6 %all-to-all-done.4 = bf16[1,32,128,128]{3,1,0,2:T(8,128)(2,1)} async-done(((bf16[1,32,128,128]{3,1,0,2:T(8,128)(2,1)}), bf16[1,32,128,128]{3,1,0,2:T(8,128)(2,1)}, u32[]{:S(2)}, u32[]{:S(2)}) %all-to-all-start.4) | async-done | bytes 1048608 | tf_op jit(solution)/shard_map/all_to_all | solution.py:84
  195.7 4.5 %all-to-all-start.5 = ((bf16[1,32,128,128]{3,1,0,2:T(8,128)(2,1)}), bf16[1,32,128,128]{3,1,0,2:T(8,128)(2,1)}, u32[]{:S(2)}, u32[]{:S(2)}) async-start(bf16[1,32,128,128]{3,1,0,2:T(8,128)(2,1)} %copy.42), calls=%async_computation.5 | async-start | bytes 2097152 | tf_op jit(solution)/shard_map/all_to_all | solution.py:85
  200.8 2.8 convolution_multiply_fusion.1
  203.6 1.1 convolution_multiply_fusion.2
  204.7 2.9 copy.40
  207.7 17.9 %all-to-all-done.5 = bf16[1,32,128,128]{3,1,0,2:T(8,128)(2,1)} async-done(((bf16[1,32,128,128]{3,1,0,2:T(8,128)(2,1)}), bf16[1,32,128,128]{3,1,0,2:T(8,128)(2,1)}, u32[]{:S(2)}, u32[]{:S(2)}) %all-to-all-start.5) | async-done | bytes 1048608 | tf_op jit(solution)/shard_map/all_to_all | solution.py:85
  225.5 1.7 copy.43
  227.4 6.3 %fusion.13 = (bf16[128,4096]{1,0:T(8,128)(2,1)S(1)}, bf16[128,4096]{1,0:T(8,128)(2,1)S(1)}, bf16[128,4096]{1,0:T(8,128)(2,1)S(1)}, bf16[128,4096]{1,0:T(8,128)(2,1)S(1)}) fusion(f32[16,8,32,128]{3,2,1,0:T(8,128)S(1)} %bitcast.153, f32[512,4096]{1,0:T(8,128)} %copy-done.1, f32[16,8,32,128]{3,2,1,0:T(8,128)S(1)} %bitcast.154), kind=kLoop, calls=%fused_computation.23 | loop fusion | flops 10485760 | bytes 16777216 | tf_op jit(solution)/shard_map/convert.13
  233.8 1.0 copy-done.17
  235.4 2.2 convolution_multiply_fusion
  237.6 3.0 fusion.31
  240.6 2.4 multiply_reduce_fusion
  243.1 3.3 multiply_convert_fusion
  246.3 37.9 %all-reduce = (f32[2,128]{1,0:T(2,128)}, f32[2,128]{1,0:T(2,128)}) all-reduce(f32[2,128]{1,0:T(2,128)S(1)} %maximum_multiply_fusion, f32[2,128]{1,0:T(2,128)S(1)} %maximum_multiply_fusion.1), channel_id=1, replica_groups=mesh['dp'=8,'dap'=4] {'dp','dap'}, use_global_device_ids=true, to_apply=%region_13.0 | all-reduce | flops 512 | bytes 4096 | tf_op jit(solution)/shard_map/psum | solution.py:110
  284.3 88.0 %all-reduce.4.cloned.1.call-done = (f32[128,512]{1,0:T(8,128)}, f32[128,128]{1,0:T(8,128)}, f32[128,128]{1,0:T(8,128)}) async-done(((f32[128,512]{1,0:T(8,128)}, f32[128,128]{1,0:T(8,128)}, f32[128,128]{1,0:T(8,128)}), (f32[128,512]{1,0:T(8,128)}, f32[128,128]{1,0:T(8,128)}, f32[128,128]{1,0:T(8,128)})) %all-reduce.4.cloned.1.call-update) | async-done | bytes 393232 | tf_op jit(solution)/shard_map/psum | solution.py:110
  372.3 1.7 copy.62
  374.0 1.5 copy.63
  375.5 1.5 copy.64
  (71 shorter events, 6.8 us)
Async XLA Ops:
  7.2 6.4 %copy-start = (bf16[128,512]{1,0:T(8,128)(2,1)S(1)}, bf16[128,512]{1,0:T(8,128)(2,1)}, u32[]{:S(2)}) copy-start(bf16[128,512]{1,0:T(8,128)(2,1)} %param.13) | copy-start | bytes 393220
  7.2 4.1 %copy-start.2 = (bf16[1,32,128,128]{3,2,1,0:T(8,128)(2,1)S(1)}, bf16[1,32,128,128]{3,2,1,0:T(8,128)(2,1)}, u32[]{:S(2)}) copy-start(bf16[1,32,128,128]{3,2,1,0:T(8,128)(2,1)} %param.9) | copy-start | bytes 3145732
  7.2 4.1 %copy-start.23 = (f32[128]{0:T(128)S(1)}, f32[128]{0:T(128)}, u32[]{:S(2)}) copy-start(f32[128]{0:T(128)} %param.11) | copy-start | bytes 1540
  7.2 4.1 %copy-start.25 = (f32[128]{0:T(128)S(1)}, f32[128]{0:T(128)}, u32[]{:S(2)}) copy-start(f32[128]{0:T(128)} %param.12) | copy-start | bytes 1540
  12.6 1.0 copy-start.5
  14.8 3.2 copy-start.1
  19.3 32.1 %all-to-all-start.1 = ((bf16[4,32,32,128]{3,2,1,0:T(8,128)(2,1)}), bf16[4,32,32,128]{3,2,1,0:T(8,128)(2,1)S(1)}, u32[]{:S(2)}, u32[]{:S(2)}) async-start(bf16[4,32,32,128]{3,2,1,0:T(8,128)(2,1)} %bitcast.157), calls=%async_computation.1 | async-start | bytes 2097152 | tf_op jit(solution)/shard_map/all_to_all | solution.py:59
  51.4 29.6 %all-to-all-start = ((bf16[4,32,32,128]{3,2,1,0:T(8,128)(2,1)}), bf16[4,32,32,128]{3,2,1,0:T(8,128)(2,1)}, u32[]{:S(2)}, u32[]{:S(2)}) async-start(bf16[4,32,32,128]{3,2,1,0:T(8,128)(2,1)} %bitcast.156), calls=%async_computation | async-start | bytes 2097152 | tf_op jit(solution)/shard_map/all_to_all | solution.py:58
  55.8 27.4 %copy-start.10 = (bf16[1,32,4,32,128]{4,3,2,1,0:T(8,128)(2,1)}, bf16[1,32,4,32,128]{4,3,2,1,0:T(8,128)(2,1)S(1)}, u32[]{:S(2)}) copy-start(bf16[1,32,4,32,128]{4,3,2,1,0:T(8,128)(2,1)S(1)} %copy.33) | copy-start | bytes 3145732
  82.3 1.6 copy-start.8
  117.5 2.0 copy-start.22
  117.5 2.0 copy-start.24
  119.4 3.3 copy-start.20
  121.7 1.0 copy-start.12
  122.7 1.2 copy-start.6
  122.7 1.2 copy-start.21
  122.8 1.6 copy-start.26
  127.0 2.4 copy-start.16
  129.4 1.4 copy-start.3
  136.6 27.9 %copy-start.11 = (bf16[1,32,4,32,128]{4,3,2,1,0:T(8,128)(2,1)S(1)}, bf16[1,32,4,32,128]{4,3,2,1,0:T(8,128)(2,1)}, u32[]{:S(2)}) copy-start(bf16[1,32,4,32,128]{4,3,2,1,0:T(8,128)(2,1)} %copy-done.10) | copy-start | bytes 3145732
  165.0 5.9 %copy-start.9 = (bf16[1,32,4,32,128]{4,3,2,1,0:T(8,128)(2,1)S(1)}, bf16[1,32,4,32,128]{4,3,2,1,0:T(8,128)(2,1)}, u32[]{:S(2)}) copy-start(bf16[1,32,4,32,128]{4,3,2,1,0:T(8,128)(2,1)} %copy-done.8) | copy-start | bytes 3145732
  166.6 29.1 %all-to-all-start.4 = ((bf16[1,32,128,128]{3,1,0,2:T(8,128)(2,1)}), bf16[1,32,128,128]{3,1,0,2:T(8,128)(2,1)}, u32[]{:S(2)}, u32[]{:S(2)}) async-start(bf16[1,32,128,128]{3,1,0,2:T(8,128)(2,1)} %copy.39), calls=%async_computation.4 | async-start | bytes 2097152 | tf_op jit(solution)/shard_map/all_to_all | solution.py:84
  171.4 28.8 %copy-start.4 = (f32[4096,128]{1,0:T(8,128)S(1)}, f32[4096,128]{1,0:T(8,128)}, u32[]{:S(2)}) copy-start(f32[4096,128]{1,0:T(8,128)} %copy-done.3) | copy-start | bytes 6291460
  195.7 29.8 %all-to-all-start.5 = ((bf16[1,32,128,128]{3,1,0,2:T(8,128)(2,1)}), bf16[1,32,128,128]{3,1,0,2:T(8,128)(2,1)}, u32[]{:S(2)}, u32[]{:S(2)}) async-start(bf16[1,32,128,128]{3,1,0,2:T(8,128)(2,1)} %copy.42), calls=%async_computation.5 | async-start | bytes 2097152 | tf_op jit(solution)/shard_map/all_to_all | solution.py:85
  200.2 172.1 %all-reduce.4.cloned.1.call-start = ((), (), s32[]{:S(2)}) async-start(), calls=%async_computation.6 | async-start | bytes 786432 | tf_op jit(solution)/shard_map/psum | solution.py:110
  200.8 2.8 copy-start.7
  200.8 2.8 copy-start.14
  225.5 1.9 copy-start.13
  233.7 1.0 copy-start.17
  233.8 1.3 copy-start.18
  233.8 1.6 copy-start.19
  237.6 3.0 copy-start.15
Sparse Core Ops, SparseCore 0:
  243.2 129.0 all-reduce.3
where the time goes:
time: 385 us; the launch traced here: 384 us
  waiting for transfers between devices  178 us (46%)
  blocking collectives  93.5 us (24%)
  local copies, waits for them, and re-layouts  32.7 us (8%)
  other arithmetic  25.3 us (7%)
  matrix products  20.1 us (5%)
  starting transfers between devices  19.4 us (5%)
  between operations  14.6 us (4%)
    psum x1, waiting for transfers between devices, shards(): lax.psum((proj_part, gate_part, out_part, in_norm_part, out_norm_part), (...  88 us
    psum x1, blocking collectives, shards(): lax.psum((proj_part, gate_part, out_part, in_norm_part, out_norm_part), (...  37.9 us
    all_to_all x1, blocking collectives, shards(): lax.all_to_all(d_tri, 'dap', split_axis=0, concat_axis=2, tiled=True)  27.8 us
    all_to_all x1, blocking collectives, shards(): lax.all_to_all(product, 'dap', split_axis=2, concat_axis=0, tiled=True)  27.7 us
    all_to_all x1, waiting for transfers between devices, shards(): lax.all_to_all(left_act, 'dap', split_axis=0, concat_axis=2, tiled=True)  25.2 us
    all_to_all x1, waiting for transfers between devices, shards(): lax.all_to_all(right_act, 'dap', split_axis=0, concat_axis=2, tiled=True)  24.5 us
    all_to_all x1, waiting for transfers between devices, shards(): lax.all_to_all(back_l, 'dap', split_axis=2, concat_axis=0, tiled=True)  22.6 us
    unnamed x61, local copies, waits for them, and re-layouts  18.7 us
  transfers between devices with their start and end apart: 5, of which 5 were waited for; matrix products, arithmetic and copies ran while one was open for 4% of the time, Pallas kernels for 0%

commit v1 on v0

--- a/solution.py
+++ b/solution.py
@@ -4,6 +4,11 @@
 from jax.sharding import PartitionSpec as P
 
 epsilon = 1e-05
+
+
+def axis_by_axis(x, one, other):
+    partial = lax.psum(x, one)
+    return lax.psum(partial, other)
 
 
 def norm_rows(values, along):
@@ -107,8 +112,8 @@
         .astype(bf16)
         .reshape(1, row_count, crop_len, channels)
     )
-    proj_sum, gate_sum, out_sum, in_sum, outn_sum = lax.psum(
-        (proj_part, gate_part, out_part, in_norm_part, out_norm_part), ("dp", "dap")
+    proj_sum, gate_sum, out_sum, in_sum, outn_sum = axis_by_axis(
+        (proj_part, gate_part, out_part, in_norm_part, out_norm_part), "dap", "dp"
     )
     return (update, pair_grad, proj_sum, gate_sum, out_sum, in_sum, outn_sum)
 

time: 385 us -> 350 us (0.909)
  waiting for transfers between devices: 178 us -> 158 us
  blocking collectives: 93.5 us -> 78.1 us
    psum x1 -> x2, waiting for transfers between devices: 88 us -> 68.2 us  [the longest x1 36.4 us: axis_by_axis(): partial = lax.psum(x, one)]
    psum x1 -> x2, blocking collectives: 37.9 us -> 22.6 us  [the longest x1 12.3 us: axis_by_axis(): return lax.psum(partial, other)]
  transfers between devices with their start and end apart: 5 -> 6, of which waited for: 5 -> 6; matrix products, arithmetic and copies ran while one was open for 4% -> 4% of each run, Pallas kernels for 0% -> 0%
where the time goes in v1:
time: 350 us; the launch traced here: 349 us
  waiting for transfers between devices  158 us (45%)
  blocking collectives  78.1 us (22%)
  local copies, waits for them, and re-layouts  32.7 us (9%)
  other arithmetic  25.3 us (7%)
  matrix products  20.1 us (6%)
  starting transfers between devices  19.4 us (6%)
  between operations  14.6 us (4%)
    psum x1, waiting for transfers between devices, axis_by_axis(): partial = lax.psum(x, one)  36.4 us
    psum x1, waiting for transfers between devices, axis_by_axis(): return lax.psum(partial, other)  31.8 us
    all_to_all x1, blocking collectives, shards(): lax.all_to_all(d_tri, 'dap', split_axis=0, concat_axis=2, tiled=True)  27.8 us
    all_to_all x1, blocking collectives, shards(): lax.all_to_all(product, 'dap', split_axis=2, concat_axis=0, tiled=True)  27.7 us
    all_to_all x1, waiting for transfers between devices, shards(): lax.all_to_all(left_act, 'dap', split_axis=0, concat_axis=2, tiled=True)  25.2 us
    all_to_all x1, waiting for transfers between devices, shards(): lax.all_to_all(right_act, 'dap', split_axis=0, concat_axis=2, tiled=True)  24.5 us
    all_to_all x1, waiting for transfers between devices, shards(): lax.all_to_all(back_l, 'dap', split_axis=2, concat_axis=0, tiled=True)  22.6 us
    unnamed x61, local copies, waits for them, and re-layouts  18.7 us
  transfers between devices with their start and end apart: 6, of which 6 were waited for; matrix products, arithmetic and copies ran while one was open for 4% of the time, Pallas kernels for 0%

profile of v1, /device:TPU:0, one launch (start us, length us, event | category | flops | bytes accessed | tf_op | source)
XLA Modules:
  0.0 348.7 jit_solution(7741343542895835444)
XLA Ops:
  7.2 1.7 convert_reduce_fusion
  8.9 2.3 multiply_reduce_fusion.3
  11.3 1.3 add_convert_fusion.1
  13.5 1.3 convolution_bitcast_fusion
  14.8 1.1 fusion.30
  15.9 2.1 copy-done.1
  18.1 1.2 copy.46
  19.3 6.3 %all-to-all-start.1 = ((bf16[4,32,32,128]{3,2,1,0:T(8,128)(2,1)}), bf16[4,32,32,128]{3,2,1,0:T(8,128)(2,1)S(1)}, u32[]{:S(2)}, u32[]{:S(2)}) async-start(bf16[4,32,32,128]{3,2,1,0:T(8,128)(2,1)} %bitcast.157), calls=%async_computation.1 | async-start | bytes 2097152 | tf_op jit(solution)/shard_map/all_to_all | solution.py:64
  25.6 1.2 copy.45
  26.8 24.5 %all-to-all-done.1 = bf16[4,32,32,128]{3,2,1,0:T(8,128)(2,1)S(1)} async-done(((bf16[4,32,32,128]{3,2,1,0:T(8,128)(2,1)}), bf16[4,32,32,128]{3,2,1,0:T(8,128)(2,1)S(1)}, u32[]{:S(2)}, u32[]{:S(2)}) %all-to-all-start.1) | async-done | bytes 1048608 | tf_op jit(solution)/shard_map/all_to_all | solution.py:64
  51.4 4.3 %all-to-all-start = ((bf16[4,32,32,128]{3,2,1,0:T(8,128)(2,1)}), bf16[4,32,32,128]{3,2,1,0:T(8,128)(2,1)}, u32[]{:S(2)}, u32[]{:S(2)}) async-start(bf16[4,32,32,128]{3,2,1,0:T(8,128)(2,1)} %bitcast.156), calls=%async_computation | async-start | bytes 2097152 | tf_op jit(solution)/shard_map/all_to_all | solution.py:63
  55.8 25.2 %all-to-all-done = bf16[4,32,32,128]{3,2,1,0:T(8,128)(2,1)} async-done(((bf16[4,32,32,128]{3,2,1,0:T(8,128)(2,1)}), bf16[4,32,32,128]{3,2,1,0:T(8,128)(2,1)}, u32[]{:S(2)}, u32[]{:S(2)}) %all-to-all-start) | async-done | bytes 1048608 | tf_op jit(solution)/shard_map/all_to_all | solution.py:63
  81.0 1.3 copy.32
  83.9 27.7 %all_to_all.72 = bf16[1,32,128,128]{3,1,0,2:T(8,128)(2,1)S(1)} all-to-all(bf16[1,32,128,128]{3,1,0,2:T(8,128)(2,1)S(1)} %copy.34), channel_id=1, replica_groups=mesh['dp'=8,'dap'=4] {'dap'}, dimensions={2} | all-to-all | bytes 2097152 | tf_op jit(solution)/shard_map/all_to_all | solution.py:68
  112.2 1.1 bitcast_reduce_fusion
  113.4 1.1 fusion.23
  114.5 3.0 copy.58
  117.5 1.9 copy.36
  119.4 2.3 add_convert_fusion
  121.8 1.0 copy-done.12
  124.3 2.7 fusion.6
  127.0 2.4 fusion.21
  129.4 1.3 copy-done.3
  130.8 4.1 %multiply_convert_fusion.1 = bf16[128,4096]{0,1:T(8,128)(2,1)} fusion(f32[4096,128]{1,0:T(8,128)S(1)} %get-tuple-element.39, f32[128,4096]{0,1:T(8,128)S(1)} %copy.36, f32[4096]{0:T(1024)S(1)} %get-tuple-element.41, f32[4096]{0:T(1024)S(1)} %get-tuple-element.42, f32[128]{0:T(128)S(1)} %copy-done.22, f32[4096]{0:T(1024)S(1)} %rsqrt_bitcast_fusion, ...), kind=kLoop, calls=%fused_computation.46 | loop fusion | flops 4194304 | bytes 5308928 | tf_op jit(solution)/shard_map/convert_element_type | solution.py:84
  134.8 1.5 copy.37
  136.6 27.8 %all_to_all.73 = bf16[4,32,32,128]{3,2,1,0:T(8,128)(2,1)S(1)} all-to-all(bf16[4,32,32,128]{3,2,1,0:T(8,128)(2,1)S(1)} %bitcast.159), channel_id=1, replica_groups=mesh['dp'=8,'dap'=4] {'dap'}, dimensions={0} | all-to-all | bytes 2097152 | tf_op jit(solution)/shard_map/all_to_all | solution.py:86
  165.0 1.7 copy.39
  166.6 4.3 %all-to-all-start.4 = ((bf16[1,32,128,128]{3,1,0,2:T(8,128)(2,1)}), bf16[1,32,128,128]{3,1,0,2:T(8,128)(2,1)}, u32[]{:S(2)}, u32[]{:S(2)}) async-start(bf16[1,32,128,128]{3,1,0,2:T(8,128)(2,1)} %copy.39), calls=%async_computation.4 | async-start | bytes 2097152 | tf_op jit(solution)/shard_map/all_to_all | solution.py:89
  171.4 1.7 copy.42
  173.1 22.6 %all-to-all-done.4 = bf16[1,32,128,128]{3,1,0,2:T(8,128)(2,1)} async-done(((bf16[1,32,128,128]{3,1,0,2:T(8,128)(2,1)}), bf16[1,32,128,128]{3,1,0,2:T(8,128)(2,1)}, u32[]{:S(2)}, u32[]{:S(2)}) %all-to-all-start.4) | async-done | bytes 1048608 | tf_op jit(solution)/shard_map/all_to_all | solution.py:89
  195.7 4.5 %all-to-all-start.5 = ((bf16[1,32,128,128]{3,1,0,2:T(8,128)(2,1)}), bf16[1,32,128,128]{3,1,0,2:T(8,128)(2,1)}, u32[]{:S(2)}, u32[]{:S(2)}) async-start(bf16[1,32,128,128]{3,1,0,2:T(8,128)(2,1)} %copy.42), calls=%async_computation.5 | async-start | bytes 2097152 | tf_op jit(solution)/shard_map/all_to_all | solution.py:90
  200.8 2.8 convolution_multiply_fusion.1
  203.6 1.1 convolution_multiply_fusion.2
  204.7 2.9 copy.40
  207.7 17.9 %all-to-all-done.5 = bf16[1,32,128,128]{3,1,0,2:T(8,128)(2,1)} async-done(((bf16[1,32,128,128]{3,1,0,2:T(8,128)(2,1)}), bf16[1,32,128,128]{3,1,0,2:T(8,128)(2,1)}, u32[]{:S(2)}, u32[]{:S(2)}) %all-to-all-start.5) | async-done | bytes 1048608 | tf_op jit(solution)/shard_map/all_to_all | solution.py:90
  225.5 1.7 copy.43
  227.4 6.3 %fusion.13 = (bf16[128,4096]{1,0:T(8,128)(2,1)S(1)}, bf16[128,4096]{1,0:T(8,128)(2,1)S(1)}, bf16[128,4096]{1,0:T(8,128)(2,1)S(1)}, bf16[128,4096]{1,0:T(8,128)(2,1)S(1)}) fusion(f32[16,8,32,128]{3,2,1,0:T(8,128)S(1)} %bitcast.153, f32[512,4096]{1,0:T(8,128)} %copy-done.1, f32[16,8,32,128]{3,2,1,0:T(8,128)S(1)} %bitcast.154), kind=kLoop, calls=%fused_computation.23 | loop fusion | flops 10485760 | bytes 16777216 | tf_op jit(solution)/shard_map/convert.13
  235.4 2.2 convolution_multiply_fusion
  237.6 3.0 fusion.31
  240.6 2.4 multiply_reduce_fusion
  243.1 36.4 %all-reduce.9.cloned.1.call-done = (f32[128,512]{1,0:T(8,128)}, f32[128,128]{1,0:T(8,128)}, f32[128,128]{1,0:T(8,128)}) async-done(((f32[128,512]{1,0:T(8,128)}, f32[128,128]{1,0:T(8,128)}, f32[128,128]{1,0:T(8,128)}), (f32[128,512]{1,0:T(8,128)}, f32[128,128]{1,0:T(8,128)}, f32[128,128]{1,0:T(8,128)})) %all-reduce.9.cloned.1.call-update) | async-done | bytes 393232 | tf_op jit(solution)/shard_map/psum | solution.py:10
  279.5 3.3 multiply_convert_fusion
  282.8 10.3 %all-reduce.2 = (f32[2,128]{1,0:T(2,128)S(1)}, f32[2,128]{1,0:T(2,128)S(1)}) all-reduce(f32[2,128]{1,0:T(2,128)S(1)} %maximum_multiply_fusion, f32[2,128]{1,0:T(2,128)S(1)} %maximum_multiply_fusion.1), channel_id=1, replica_groups=mesh['dp'=8,'dap'=4] {'dap'}, use_global_device_ids=true, to_apply=%region_16.0 | all-reduce | flops 512 | bytes 4096 | tf_op jit(solution)/shard_map/psum | solution.py:10
  293.1 12.3 %all-reduce = (f32[2,128]{1,0:T(2,128)}, f32[2,128]{1,0:T(2,128)}) all-reduce(f32[2,128]{1,0:T(2,128)S(1)} %get-tuple-element.19, f32[2,128]{1,0:T(2,128)S(1)} %get-tuple-element.20), channel_id=1, replica_groups=mesh['dp'=8,'dap'=4] {'dp'}, use_global_device_ids=true, to_apply=%region_17.0 | all-reduce | flops 512 | bytes 4096 | tf_op jit(solution)/shard_map/psum | solution.py:11
  305.4 31.8 %all-reduce.7.cloned.1.call-done = (f32[128,512]{1,0:T(8,128)}, f32[128,128]{1,0:T(8,128)}, f32[128,128]{1,0:T(8,128)}) async-done(((f32[128,512]{1,0:T(8,128)}, f32[128,128]{1,0:T(8,128)}, f32[128,128]{1,0:T(8,128)}), (f32[128,512]{1,0:T(8,128)}, f32[128,128]{1,0:T(8,128)}, f32[128,128]{1,0:T(8,128)})) %all-reduce.7.cloned.1.call-update) | async-done | bytes 393232 | tf_op jit(solution)/shard_map/psum | solution.py:11
  337.3 1.7 copy.65
  338.9 1.5 copy.66
  340.4 1.5 copy.67
  (75 shorter events, 8.8 us)
Async XLA Ops:
  7.2 6.4 %copy-start = (bf16[128,512]{1,0:T(8,128)(2,1)S(1)}, bf16[128,512]{1,0:T(8,128)(2,1)}, u32[]{:S(2)}) copy-start(bf16[128,512]{1,0:T(8,128)(2,1)} %param.13) | copy-start | bytes 393220
  7.2 4.1 %copy-start.2 = (bf16[1,32,128,128]{3,2,1,0:T(8,128)(2,1)S(1)}, bf16[1,32,128,128]{3,2,1,0:T(8,128)(2,1)}, u32[]{:S(2)}) copy-start(bf16[1,32,128,128]{3,2,1,0:T(8,128)(2,1)} %param.9) | copy-start | bytes 3145732
  7.2 4.1 %copy-start.23 = (f32[128]{0:T(128)S(1)}, f32[128]{0:T(128)}, u32[]{:S(2)}) copy-start(f32[128]{0:T(128)} %param.11) | copy-start | bytes 1540
  7.2 4.1 %copy-start.25 = (f32[128]{0:T(128)S(1)}, f32[128]{0:T(128)}, u32[]{:S(2)}) copy-start(f32[128]{0:T(128)} %param.12) | copy-start | bytes 1540
  12.6 1.0 copy-start.5
  14.8 3.2 copy-start.1
  19.3 32.1 %all-to-all-start.1 = ((bf16[4,32,32,128]{3,2,1,0:T(8,128)(2,1)}), bf16[4,32,32,128]{3,2,1,0:T(8,128)(2,1)S(1)}, u32[]{:S(2)}, u32[]{:S(2)}) async-start(bf16[4,32,32,128]{3,2,1,0:T(8,128)(2,1)} %bitcast.157), calls=%async_computation.1 | async-start | bytes 2097152 | tf_op jit(solution)/shard_map/all_to_all | solution.py:64
  51.4 29.6 %all-to-all-start = ((bf16[4,32,32,128]{3,2,1,0:T(8,128)(2,1)}), bf16[4,32,32,128]{3,2,1,0:T(8,128)(2,1)}, u32[]{:S(2)}, u32[]{:S(2)}) async-start(bf16[4,32,32,128]{3,2,1,0:T(8,128)(2,1)} %bitcast.156), calls=%async_computation | async-start | bytes 2097152 | tf_op jit(solution)/shard_map/all_to_all | solution.py:63
  55.8 27.4 %copy-start.10 = (bf16[1,32,4,32,128]{4,3,2,1,0:T(8,128)(2,1)}, bf16[1,32,4,32,128]{4,3,2,1,0:T(8,128)(2,1)S(1)}, u32[]{:S(2)}) copy-start(bf16[1,32,4,32,128]{4,3,2,1,0:T(8,128)(2,1)S(1)} %copy.33) | copy-start | bytes 3145732
  82.3 1.6 copy-start.8
  117.5 2.0 copy-start.22
  117.5 2.0 copy-start.24
  119.4 3.3 copy-start.20
  121.7 1.0 copy-start.12
  122.7 1.2 copy-start.6
  122.7 1.2 copy-start.21
  122.8 1.6 copy-start.26
  127.0 2.4 copy-start.16
  129.4 1.4 copy-start.3
  136.6 27.9 %copy-start.11 = (bf16[1,32,4,32,128]{4,3,2,1,0:T(8,128)(2,1)S(1)}, bf16[1,32,4,32,128]{4,3,2,1,0:T(8,128)(2,1)}, u32[]{:S(2)}) copy-start(bf16[1,32,4,32,128]{4,3,2,1,0:T(8,128)(2,1)} %copy-done.10) | copy-start | bytes 3145732
  165.0 5.9 %copy-start.9 = (bf16[1,32,4,32,128]{4,3,2,1,0:T(8,128)(2,1)S(1)}, bf16[1,32,4,32,128]{4,3,2,1,0:T(8,128)(2,1)}, u32[]{:S(2)}) copy-start(bf16[1,32,4,32,128]{4,3,2,1,0:T(8,128)(2,1)} %copy-done.8) | copy-start | bytes 3145732
  166.6 29.1 %all-to-all-start.4 = ((bf16[1,32,128,128]{3,1,0,2:T(8,128)(2,1)}), bf16[1,32,128,128]{3,1,0,2:T(8,128)(2,1)}, u32[]{:S(2)}, u32[]{:S(2)}) async-start(bf16[1,32,128,128]{3,1,0,2:T(8,128)(2,1)} %copy.39), calls=%async_computation.4 | async-start | bytes 2097152 | tf_op jit(solution)/shard_map/all_to_all | solution.py:89
  171.4 28.8 %copy-start.4 = (f32[4096,128]{1,0:T(8,128)S(1)}, f32[4096,128]{1,0:T(8,128)}, u32[]{:S(2)}) copy-start(f32[4096,128]{1,0:T(8,128)} %copy-done.3) | copy-start | bytes 6291460
  195.7 29.8 %all-to-all-start.5 = ((bf16[1,32,128,128]{3,1,0,2:T(8,128)(2,1)}), bf16[1,32,128,128]{3,1,0,2:T(8,128)(2,1)}, u32[]{:S(2)}, u32[]{:S(2)}) async-start(bf16[1,32,128,128]{3,1,0,2:T(8,128)(2,1)} %copy.42), calls=%async_computation.5 | async-start | bytes 2097152 | tf_op jit(solution)/shard_map/all_to_all | solution.py:90
  200.2 79.3 %all-reduce.9.cloned.1.call-start = ((), (), s32[]{:S(2)}) async-start(), calls=%async_computation.7 | async-start | bytes 786432 | tf_op jit(solution)/shard_map/psum | solution.py:10
  200.8 2.8 copy-start.7
  200.8 2.8 copy-start.14
  225.5 1.9 copy-start.13
  233.7 1.0 copy-start.17
  233.8 1.3 copy-start.18
  233.8 1.6 copy-start.19
  237.6 3.0 copy-start.15
  243.1 94.2 %all-reduce.7.cloned.1.call-start = ((), (), s32[]{:S(2)}) async-start(), calls=%async_computation.6 | async-start | bytes 786432 | tf_op jit(solution)/shard_map/psum | solution.py:11
Sparse Core Ops, SparseCore 0:
  243.2 36.2 all-reduce.8
  282.9 54.3 all-reduce.6
